TPU v7x, 32 devices: a whole 2x2x4 slice. The times are simulated.
32 devices in a mesh: slab: 2 (over x), scan: 8 (over z, y), mz: 2 (over core).
Axes of the slice: x: 2, y: 2, z: 4, core: 2. Of those that a mesh axis runs over, the one named last changes fastest.
Arguments:
- spectra: bfloat16 [12288, 8192], P('mz', ('slab', 'scan')), parts along dimension 1, may hold values from 0 to 1
- templates: bfloat16 [2, 12288, 512], P('mz', ('slab', 'scan')), parts along dimension 1, may hold values from 0 to 2
- activations: float32 [64, 8192], P(None, ('slab', 'scan')), parts along dimension 1, may hold values from 0 to 1
- h_rate: float32 [64], replicated, may hold values from 0.02 to 0.08
- w_rate: float32 [64], replicated, may hold values from 0.2 to 0.8
Outputs:
- new_activations: float32 [64, 8192], P(None, ('slab', 'scan')), parts along dimension 1
- new_templates: bfloat16 [2, 12288, 512], P('mz', ('slab', 'scan')), parts along dimension 1
There are 2 independent parts, one for each index of `slab`. A program takes and returns all parts, laid end to end along the dimension named above; an argument that names none is the same for every part. Nothing has to cross between parts.
All inputs are finite; a program needn't handle non-finite values.
Results may differ from a plain program's by a relative error of at most 0.00082.
Values may be sent and summed in bfloat16 or wider, within the bound.
No kernel may reach another device: no remote copies, remote signals or barrier semaphores. Data moves between devices by JAX's collectives and lax.ppermute only.
A program may use at most 128 MiB of HBM per device.

v0:
```python
import jax
import jax.numpy as jnp
from jax import lax
from jax.sharding import PartitionSpec as P

K = 64
LAGS = 8
LAG = 64
SPAN = 448


def shifted(x, axis, by):
    size = lax.axis_size(axis)
    pairs = [(i, i + by) for i in range(size) if 0 <= i + by < size]
    return lax.ppermute(x, axis, pairs)


def lagged(hb):
    width = hb.shape[1]
    tail = shifted(hb[:, width - SPAN :], "scan", 1)
    extended = jnp.concatenate([tail, hb], 1)
    return jnp.concatenate(
        [extended[:, SPAN - l * LAG : SPAN - l * LAG + width] for l in range(LAGS)], 0
    )


def lag_total(prods, count):
    width = prods.shape[1]
    after = shifted(prods[:, :SPAN], "scan", -1)
    extended = jnp.concatenate([prods, after], 1)
    total = extended[0:count, 0:width]
    for l in range(1, LAGS):
        total = total + extended[l * count : (l + 1) * count, l * LAG : l * LAG + width]
    return total


def per_device(spectra, templates, activations, h_rate, w_rate):
    scale = 1.0 / (LAGS * K)
    own_rows = templates.reshape(templates.shape[1], templates.shape[2])
    weights = lax.all_gather(own_rows, "scan", axis=0, tiled=True)
    data = spectra.astype(jnp.float32)
    stack = lagged(activations.astype(jnp.bfloat16))
    recon = scale * jnp.dot(weights, stack, preferred_element_type=jnp.float32)
    resid = (recon - data).astype(jnp.bfloat16)
    prods = lax.dot_general(
        weights, resid, (((0,), (0,)), ((), ())), preferred_element_type=jnp.float32
    )
    summed = lax.psum(prods, "mz")
    grad_h = scale * lag_total(summed, K)
    new_h = jnp.maximum(activations - h_rate[:, None] * grad_h, 0.0)
    new_hb = new_h.astype(jnp.bfloat16)
    stack_new = lagged(new_hb)
    recon_new = scale * jnp.dot(weights, stack_new, preferred_element_type=jnp.float32)
    resid_new = (recon_new - data).astype(jnp.bfloat16)
    gathered_rows = lax.all_to_all(resid_new, "scan", split_axis=0, concat_axis=1, tiled=True)
    all_h = lax.all_gather(new_hb, "scan", axis=1, tiled=True)
    total = all_h.shape[1]
    padded = jnp.pad(all_h, ((0, 0), (SPAN, 0)))
    full_stack = jnp.concatenate(
        [padded[:, SPAN - l * LAG : SPAN - l * LAG + total] for l in range(LAGS)], 0
    )
    grad_w = scale * lax.dot_general(
        gathered_rows, full_stack, (((1,), (1,)), ((), ())), preferred_element_type=jnp.float32
    )
    rates = jnp.tile(w_rate, LAGS)[None, :]
    new_w = jnp.maximum(own_rows.astype(jnp.float32) - rates * grad_w, 0.0).astype(jnp.bfloat16)
    return (new_h, new_w.reshape(templates.shape))


def solution(mesh):
    placed = (
        P("mz", ("slab", "scan")),
        P("mz", ("slab", "scan"), None),
        P(None, ("slab", "scan")),
        P(),
        P(),
    )
    return jax.shard_map(
        per_device,
        mesh=mesh,
        in_specs=placed,
        out_specs=(P(None, ("slab", "scan")), P("mz", ("slab", "scan"), None)),
        check_vma=False,
    )
```

profile of v0, /device:TPU:0, one launch (start us, length us, event | category | flops | bytes accessed | tf_op | source)
XLA Modules:
  0.0 383.2 jit_solution(8813983667833982358)
XLA Ops:
  7.2 0.0 all-gather.3.cloned.1.call-start
  7.2 0.7 all-gather.3.cloned.1.call-update
  7.9 0.0 all-reduce.3.cloned.1.call-start
  7.9 0.9 constant_dynamic-update-slice_fusion
  8.9 0.1 slice.129
  9.0 4.9 %collective-permute-start = (bf16[64,448]{1,0:T(8,128)(2,1)S(1)}, bf16[64,448]{1,0:T(8,128)(2,1)S(1)}, u32[]{:S(2)}, u32[]{:S(2)}) collective-permute-start(bf16[64,448]{1,0:T(8,128)(2,1)S(1)} %slice.129), channel_id=1, source_target_pairs={{0,2},{2,4},{4,6},{6,8},{8,10},{10,12},{12,14},{1,3},{3,5},{5,7},{... | collective-permute-start | bytes 172040 | tf_op jit(solution)/shard_map/ppermute | solution.py:15
  13.9 8.8 %copy.10 = bf16[6144,512]{0,1:T(8,128)(2,1)} copy(bf16[6144,512]{1,0:T(8,128)(2,1)} %param.5) | data formatting | bytes 12582912 | tf_op args[0]
  22.7 0.0 collective-permute-done
  22.7 0.1 fusion.28
  22.7 0.1 fusion.30
  22.8 0.1 fusion.32
  22.9 0.1 fusion.34
  23.0 0.1 fusion.36
  23.1 0.1 fusion.26
  23.2 0.1 fusion.37
  23.3 0.0 copy-start
  23.3 0.0 copy-start.1
  23.3 88.3 %all-gather.3.cloned.1.call-done = bf16[1,6144,512]{2,1,0:T(8,128)(2,1)} async-done(((bf16[1,768,512]{2,1,0:T(8,128)(2,1)}), bf16[1,6144,512]{2,1,0:T(8,128)(2,1)}) %all-gather.3.cloned.1.call-update) | async-done | bytes 6291472 | tf_op jit(solution)/shard_map/all_gather | solution.py:40
  111.6 14.2 %fusion.10 = f32[512,512]{0,1:T(8,128)} fusion(bf16[1,6144,512]{2,1,0:T(8,128)(2,1)} %all-gather.3.cloned.1.call-done, bf16[6144,512]{0,1:T(8,128)(2,1)} %copy.10, bf16[512,512]{1,0:T(8,128)(2,1)S(1)} %fusion.37), kind=kOutput, calls=%fused_computation.12 | convolution fusion | flops 6455033856 | bytes 14155776 | tf_op jit(solution)/shard_map/dot_general | solution.py:45
  125.8 0.0 all-reduce.3.cloned.1.call-update
  125.8 17.7 %all-reduce.3.cloned.1.call-done = f32[512,512]{0,1:T(8,128)} async-done(((f32[512,512]{0,1:T(8,128)}), f32[512,512]{0,1:T(8,128)}) %all-reduce.3.cloned.1.call-update) | async-done | bytes 1048592 | tf_op jit(solution)/shard_map/psum | solution.py:48
  143.5 1.2 slice.143
  144.8 1.3 collective-permute-start.1
  146.1 0.0 copy-done
  146.1 0.1 copy.11
  146.2 0.0 copy-done.1
  146.2 1.3 constant_dynamic-update-slice_fusion.2
  147.5 21.7 %collective-permute-done.1 = f32[512,448]{0,1:T(8,128)S(1)} collective-permute-done((f32[512,448]{0,1:T(8,128)S(1)}, f32[512,448]{0,1:T(8,128)S(1)}, u32[]{:S(2)}, u32[]{:S(2)}) %collective-permute-start.1) | collective-permute-done | bytes 917536 | tf_op jit(solution)/shard_map/ppermute | solution.py:15
  169.2 0.1 constant_dynamic-update-slice_fusion.1
  169.3 1.3 fusion.39
  170.6 4.5 %collective-permute-start.2 = (bf16[64,448]{0,1:T(8,128)(2,1)S(1)}, bf16[64,448]{0,1:T(8,128)(2,1)S(1)}, u32[]{:S(2)}, u32[]{:S(2)}) collective-permute-start(bf16[64,448]{0,1:T(8,128)(2,1)S(1)} %slice.151), channel_id=1, source_target_pairs={{0,2},{2,4},{4,6},{6,8},{8,10},{10,12},{12,14},{1,3},{3,5},{5,7},{... | collective-permute-start | bytes 172040 | tf_op jit(solution)/shard_map/ppermute | solution.py:15
  175.2 2.3 collective-permute-done.2
  177.5 0.1 pad_maximum_fusion
  177.6 0.5 concatenate.22
  178.1 7.5 %fusion.1 = bf16[6144,512]{0,1:T(8,128)(2,1)S(1)} fusion(bf16[6144,512]{0,1:T(8,128)(2,1)} %copy.10, bf16[512,512]{0,1:T(8,128)(2,1)S(1)} %concatenate.22, bf16[1,6144,512]{2,1,0:T(8,128)(2,1)} %all-gather.3.cloned.1.call-done), kind=kOutput, calls=%fused_computation.3 | convolution fusion | flops 3233808384 | bytes 19398656 | tf_op jit(solution)/shard_map/dot_general | solution.py:53
  185.6 3.1 copy.16
  188.7 0.0 copy-start.2
  188.7 5.7 %all-to-all-start = ((bf16[8,768,512]{1,2,0:T(8,128)(2,1)}), bf16[8,768,512]{1,2,0:T(8,128)(2,1)}, u32[]{:S(2)}, u32[]{:S(2)}) async-start(bf16[8,768,512]{1,2,0:T(8,128)(2,1)} %bitcast.39), calls=%async_computation | async-start | bytes 12582912 | tf_op jit(solution)/shard_map/all_to_all | solution.py:55
  194.3 0.0 copy-done.2
  194.4 0.1 mul.49
  194.5 0.8 copy.13
  195.2 158.4 %all_gather.7 = bf16[64,4096]{0,1:T(8,128)(2,1)S(1)} all-gather(bf16[64,512]{0,1:T(8,128)(2,1)S(1)} %get-tuple-element.6), channel_id=1, replica_groups=mesh['slab'=2,'scan'=8,'mz'=2] {'scan'}, dimensions={1}, use_global_device_ids=true | all-gather | bytes 589824 | tf_op jit(solution)/shard_map/all_gather | solution.py:56
  353.7 3.6 pad_slice_fusion
  357.3 10.5 %concatenate.23 = bf16[512,4096]{0,1:T(8,128)(2,1)} concatenate(bf16[64,4096]{0,1:T(8,128)(2,1)S(1)} %all_gather.7, bf16[64,4096]{0,1:T(8,128)(2,1)} %get-tuple-element.16, bf16[64,4096]{0,1:T(8,128)(2,1)S(1)} %get-tuple-element.11, bf16[64,4096]{0,1:T(8,128)(2,1)} %get-tuple-element.12, bf16[64,4096]{0,1:T(8,128)(2,1)} %get-tuple-element.13, ...), dimensions={0} | concatenate | bytes 8388608 | tf_op jit(solution)/shard_map/concatenate | solution.py:59
  367.8 0.0 all-to-all-done
  367.8 8.5 %fusion.15 = bf16[1,768,512]{2,1,0:T(8,128)(2,1)} fusion(bf16[768,4096]{0,1:T(8,128)(2,1)} %bitcast.6, bf16[512,4096]{0,1:T(8,128)(2,1)} %concatenate.23, bf16[1,768,512]{2,1,0:T(8,128)(2,1)} %param.6, f32[512]{0:T(512)S(1)} %mul.49), kind=kOutput, calls=%fused_computation.13 | convolution fusion | flops 3223191552 | bytes 12060672 | tf_op jit(solution)/shard_map/dot_general | solution.py:62
  (4 shorter events, 0.0 us)
Async XLA Ops:
  7.2 104.4 %all-gather.3.cloned.1.call-start = ((), (), s32[]{:S(2)}) async-start(), calls=%async_computation.2 | async-start | bytes 7077888 | tf_op jit(solution)/shard_map/all_gather | solution.py:40
  7.9 135.6 %all-reduce.3.cloned.1.call-start = ((), (), s32[]{:S(2)}) async-start(), calls=%async_computation.1 | async-start | bytes 2097152 | tf_op jit(solution)/shard_map/psum | solution.py:48
  9.0 13.7 %collective-permute-start = (bf16[64,448]{1,0:T(8,128)(2,1)S(1)}, bf16[64,448]{1,0:T(8,128)(2,1)S(1)}, u32[]{:S(2)}, u32[]{:S(2)}) collective-permute-start(bf16[64,448]{1,0:T(8,128)(2,1)S(1)} %slice.129), channel_id=1, source_target_pairs={{0,2},{2,4},{4,6},{6,8},{8,10},{10,12},{12,14},{1,3},{3,5},{5,7},{... | collective-permute-start | bytes 172040 | tf_op jit(solution)/shard_map/ppermute | solution.py:15
  23.3 122.8 %copy-start = (f32[64,512]{1,0:T(8,128)S(1)}, f32[64,512]{1,0:T(8,128)}, u32[]{:S(2)}) copy-start(f32[64,512]{1,0:T(8,128)} %param.7) | copy-start | bytes 393220
  23.3 122.9 %copy-start.1 = (f32[64]{0:T(128)S(1)}, f32[64]{0:T(128)}, u32[]{:S(2)}) copy-start(f32[64]{0:T(128)} %param.8) | copy-start | bytes 772
  144.8 24.4 %collective-permute-start.1 = (f32[512,448]{0,1:T(8,128)S(1)}, f32[512,448]{0,1:T(8,128)S(1)}, u32[]{:S(2)}, u32[]{:S(2)}) collective-permute-start(f32[512,448]{0,1:T(8,128)S(1)} %slice.143), channel_id=1, source_target_pairs={{2,0},{4,2},{6,4},{8,6},{10,8},{12,10},{14,12},{3,1},{5,3},{7,5},{... | collective-permute-start | bytes 2752520 | tf_op jit(solution)/shard_map/ppermute | solution.py:15
  170.6 6.9 %collective-permute-start.2 = (bf16[64,448]{0,1:T(8,128)(2,1)S(1)}, bf16[64,448]{0,1:T(8,128)(2,1)S(1)}, u32[]{:S(2)}, u32[]{:S(2)}) collective-permute-start(bf16[64,448]{0,1:T(8,128)(2,1)S(1)} %slice.151), channel_id=1, source_target_pairs={{0,2},{2,4},{4,6},{6,8},{8,10},{10,12},{12,14},{1,3},{3,5},{5,7},{... | collective-permute-start | bytes 172040 | tf_op jit(solution)/shard_map/ppermute | solution.py:15
  188.7 5.7 %copy-start.2 = (f32[64]{0:T(128)S(1)}, f32[64]{0:T(128)}, u32[]{:S(2)}) copy-start(f32[64]{0:T(128)} %param.9) | copy-start | bytes 772
  188.7 179.1 %all-to-all-start = ((bf16[8,768,512]{1,2,0:T(8,128)(2,1)}), bf16[8,768,512]{1,2,0:T(8,128)(2,1)}, u32[]{:S(2)}, u32[]{:S(2)}) async-start(bf16[8,768,512]{1,2,0:T(8,128)(2,1)} %bitcast.39), calls=%async_computation | async-start | bytes 12582912 | tf_op jit(solution)/shard_map/all_to_all | solution.py:55
Sparse Core Ops, SparseCore 0:
  10.2 101.4 all-gather.2
  125.9 17.5 all-reduce.2
where the time goes:
time: 384 us; the launch traced here: 383 us
  blocking collectives  158 us (41%)
  waiting for transfers between devices  131 us (34%)
  local copies, waits for them, and re-layouts  30.1 us (8%)
  matrix products  30.1 us (8%)
  starting transfers between devices  16.5 us (4%)
  between operations  14.2 us (4%)
    all_gather x1, blocking collectives, per_device(): all_h = lax.all_gather(new_hb, 'scan', axis=1, tiled=True)  158 us
    all_gather x1, waiting for transfers between devices, per_device(): weights = lax.all_gather(own_rows, 'scan', axis=0, tiled=True)  88.3 us
    ppermute x3, waiting for transfers between devices, shifted(): return lax.ppermute(x, axis, pairs)  24 us
    psum x1, waiting for transfers between devices, per_device(): summed = lax.psum(prods, 'mz')  17.7 us
    dot_general x1, matrix products, per_device(): lax.dot_general(weights, resid, (((0,), (0,)), ((), ())), preferred_eleme...  14.2 us
    unnamed x10, local copies, waits for them, and re-layouts  11 us
    ppermute x3, starting transfers between devices, shifted(): return lax.ppermute(x, axis, pairs)  10.7 us
    concatenate x1, local copies, waits for them, and re-layouts, per_device(): jnp.concatenate([padded[:, SPAN - l * LAG:SPAN - l * LAG + total] for l i...  10.5 us
  transfers between devices with their start and end apart: 6, of which 4 were waited for; matrix products, arithmetic and copies ran while one was open for 7% of the time, Pallas kernels for 0%

commit v1 on v0

v1 whole, which is shorter than its diff:
```python
import functools
import math

import jax
import jax.numpy as jnp
from jax import lax
from jax.experimental import pallas as pl
from jax.experimental.pallas import tpu as pltpu
from jax.sharding import PartitionSpec as P

LAG = 64
PAIR = 2 * LAG

SWAP = [(0, 1), (1, 0)]


def aligned(start):
    return pl.multiple_of(start, PAIR)


def row_tile(rows):
    return rows if rows <= 256 else math.gcd(rows, 256)


def fill_stack(core, mine, other, pairs, pad):
    blocks, comps, half = mine.shape
    pairs[:, :pad] = jnp.zeros((2 * comps, pad), pairs.dtype)

    def put(first, second):
        def one(b, _):
            at = pad + b * 2 * half
            pairs[:comps, pl.ds(aligned(at), half)] = first[b]
            pairs[:comps, pl.ds(aligned(at + half), half)] = second[b]
            return 0

        lax.fori_loop(0, blocks, one, 0)

    @pl.when(core == 0)
    def _():
        put(mine, other)

    @pl.when(core == 1)
    def _():
        put(other, mine)

    width = 2 * half

    def shift(b, _):
        at = pad + b * width
        wide = pairs[:comps, pl.ds(aligned(at - PAIR), width + PAIR)]
        pairs[comps:, pl.ds(aligned(at), width)] = wide[:, PAIR - LAG : PAIR - LAG + width]
        return 0

    lax.fori_loop(0, blocks, shift, 0)


def lagged_tile(pairs, start, width, count):
    return jnp.concatenate(
        [pairs[:, pl.ds(aligned(start - p * PAIR), width)] for p in range(count)], 0
    )


def first_kernel(scale, pad, core, w, wt, mine, other, data, out, pairs, total, resid):
    j = pl.program_id(0)
    blocks = pl.num_programs(0)
    rows, lagrows = w.shape
    comps = mine.shape[1]
    width = data.shape[2]
    count = lagrows // (2 * comps)

    @pl.when(j == 0)
    def _():
        fill_stack(core[0], mine, other, pairs, pad)
        total[...] = jnp.zeros_like(total)

    at = pad + j * width
    stack = lagged_tile(pairs, at, width, count)
    tile = row_tile(rows)
    for r in range(0, rows, tile):
        recon = jnp.dot(w[r : r + tile, :], stack, preferred_element_type=jnp.float32)
        resid[r : r + tile, :] = (
            scale * recon - data[0, r : r + tile, :].astype(jnp.float32)
        ).astype(jnp.bfloat16)
    for p in range(count):
        prods = jnp.dot(
            wt[p * 2 * comps : (p + 1) * 2 * comps, :], resid[...], preferred_element_type=jnp.float32
        )
        total[:, pl.ds(aligned(at - p * PAIR), width)] += prods

    @pl.when(j == blocks - 1)
    def _():
        half = width // 2

        def one(b, _):
            for h in range(2):
                start = pad + b * width + h * half
                wide = total[comps:, pl.ds(aligned(start), half + PAIR)]
                out[h, b] = total[:comps, pl.ds(aligned(start), half)] + wide[:, LAG : LAG + half]
            return 0

        lax.fori_loop(0, out.shape[1], one, 0)


def second_kernel(scale, pad, core, w, rates, mine, other, data, out, pairs, total):
    j = pl.program_id(0)
    blocks = pl.num_programs(0)
    rows, lagrows = w.shape
    comps = mine.shape[1]
    width = data.shape[2]
    count = lagrows // (2 * comps)

    @pl.when(j == 0)
    def _():
        fill_stack(core[0], mine, other, pairs, pad)
        total[...] = jnp.zeros_like(total)

    stack = lagged_tile(pairs, pad + j * width, width, count)
    tile = row_tile(rows)
    for r in range(0, rows, tile):
        recon = jnp.dot(w[r : r + tile, :], stack, preferred_element_type=jnp.float32)
        resid = (scale * recon - data[0, r : r + tile, :].astype(jnp.float32)).astype(jnp.bfloat16)
        total[r : r + tile, :] += lax.dot_general(
            resid, stack, (((1,), (1,)), ((), ())), preferred_element_type=jnp.float32
        )

    @pl.when(j == blocks - 1)
    def _():
        for r in range(0, rows, tile):
            kept = w[r : r + tile, :].astype(jnp.float32)
            out[r : r + tile, :] = jnp.maximum(
                kept - rates[...] * (scale * total[r : r + tile, :]), 0.0
            ).astype(jnp.bfloat16)


def whole(shape):
    return pl.BlockSpec(shape, lambda j: (0,) * len(shape))


def gathered(x, count):
    copies = jnp.broadcast_to(x[None], (count,) + x.shape)
    return lax.all_to_all(copies, "scan", 0, 0, tiled=True)


def per_device(spectra, templates, activations, h_rate, w_rate):
    count = lax.axis_size("scan")
    core = lax.axis_index("mz")
    rows, lagrows = templates.shape[1:]
    comps, width = activations.shape
    half = width // 2
    scale = 1.0 / lagrows
    lags = lagrows // comps
    pad = -(-lags * LAG // PAIR) * PAIR
    core_id = core.astype(jnp.int32)[None]

    own = templates.reshape(rows, lagrows)
    own_t = own.T
    act_half = lax.dynamic_slice(activations, (0, core * half), (comps, half))
    mine = gathered(act_half.astype(jnp.bfloat16), count)
    other = lax.ppermute(mine, "mz", SWAP)
    data = lax.all_to_all(spectra.reshape(count, rows, width), "scan", 0, 0, tiled=True)

    stack_shape = pltpu.VMEM((2 * comps, pad + count * width), jnp.bfloat16)
    smem = pl.BlockSpec(memory_space=pltpu.SMEM)
    flops = 4 * rows * lagrows * width * count
    cost = pl.CostEstimate(
        flops=flops, bytes_accessed=2 * rows * width * count, transcendentals=0
    )
    partial = pl.pallas_call(
        functools.partial(first_kernel, scale, pad),
        grid=(count,),
        out_shape=jax.ShapeDtypeStruct((2, count, comps, half), jnp.float32),
        in_specs=[
            smem,
            whole((rows, lagrows)),
            whole((lagrows, rows)),
            whole((count, comps, half)),
            whole((count, comps, half)),
            pl.BlockSpec((1, rows, width), lambda j: (j, 0, 0)),
        ],
        out_specs=whole((2, count, comps, half)),
        scratch_shapes=[
            stack_shape,
            pltpu.VMEM((2 * comps, pad + count * width + PAIR), jnp.float32),
            pltpu.VMEM((rows, width), jnp.bfloat16),
        ],
        cost_estimate=cost,
        compiler_params=pltpu.CompilerParams(dimension_semantics=("arbitrary",)),
        name="first",
    )(core_id, own, own_t, mine, other, data)

    keep = lax.dynamic_index_in_dim(partial, core, 0, keepdims=False)
    give = lax.dynamic_index_in_dim(partial, 1 - core, 0, keepdims=False)
    both = keep + lax.ppermute(give, "mz", SWAP)
    pieces = lax.all_to_all(both, "scan", 0, 0, tiled=True)
    grad = scale * jnp.sum(pieces, 0)
    new_half = jnp.maximum(act_half - h_rate[:, None] * grad, 0.0)
    mine_new = gathered(new_half.astype(jnp.bfloat16), count)
    other_new = lax.ppermute(mine_new, "mz", SWAP)
    new_other = lax.ppermute(new_half, "mz", SWAP)
    new_h = jnp.where(
        core == 0,
        jnp.concatenate([new_half, new_other], 1),
        jnp.concatenate([new_other, new_half], 1),
    )

    rates = jnp.tile(w_rate, lags)[None, :]
    new_w = pl.pallas_call(
        functools.partial(second_kernel, scale, pad),
        grid=(count,),
        out_shape=jax.ShapeDtypeStruct((rows, lagrows), jnp.bfloat16),
        in_specs=[
            smem,
            whole((rows, lagrows)),
            whole((1, lagrows)),
            whole((count, comps, half)),
            whole((count, comps, half)),
            pl.BlockSpec((1, rows, width), lambda j: (j, 0, 0)),
        ],
        out_specs=whole((rows, lagrows)),
        scratch_shapes=[stack_shape, pltpu.VMEM((rows, lagrows), jnp.float32)],
        cost_estimate=cost,
        compiler_params=pltpu.CompilerParams(dimension_semantics=("arbitrary",)),
        name="second",
    )(core_id, own, rates, mine_new, other_new, data)
    return (new_h, new_w.reshape(templates.shape))


def solution(mesh):
    placed = (
        P("mz", ("slab", "scan")),
        P("mz", ("slab", "scan"), None),
        P(None, ("slab", "scan")),
        P(),
        P(),
    )
    return jax.shard_map(
        per_device,
        mesh=mesh,
        in_specs=placed,
        out_specs=(P(None, ("slab", "scan")), P("mz", ("slab", "scan"), None)),
        check_vma=False,
    )
```

time: 384 us -> 226 us (0.59)
  blocking collectives: 158 us -> 28.5 us
  matrix products: 30.1 us -> 0 us
  Pallas kernels: 0 us -> 27.3 us
  local copies, waits for them, and re-layouts: 30.1 us -> 4.52 us
  waiting for transfers between devices: 131 us -> 153 us
  between operations: 14.2 us -> 0.74 us
  starting transfers between devices: 16.5 us -> 9.2 us
    all_gather x1 -> x0, blocking collectives: 158 us -> none  [per_device(): all_h = lax.all_gather(new_hb, 'scan', axis=1, tiled=True)]
    all_to_all x1 -> x2, waiting for transfers between devices: 0.01 us -> 150 us  [the longest x1 135 us: per_device(): lax.all_to_all(spectra.reshape(count, rows, width), 'scan', 0, 0, tiled=T...]
    all_gather x1 -> x0, waiting for transfers between devices: 88.3 us -> none  [per_device(): weights = lax.all_gather(own_rows, 'scan', axis=0, tiled=True)]
    dot_general x3 -> x0, matrix products: 30.1 us -> none  [the longest x1 14.2 us: per_device(): lax.dot_general(weights, resid, (((0,), (0,)), ((), ())), preferred_eleme...]
    all_to_all x0 -> x2, blocking collectives: none -> 28.5 us  [gathered(): return lax.all_to_all(copies, 'scan', 0, 0, tiled=True)]
    pallas_call x0 -> x2, Pallas kernels: none -> 27.3 us  [the longest x1 13.7 us: per_device(): pl.pallas_call(functools.partial(second_kernel, scale, pad), grid=(count,...]
    ppermute x3 -> x4, waiting for transfers between devices: 24 us -> 2.7 us  [the longest x1 1.9 us: per_device(): both = keep + lax.ppermute(give, 'mz', SWAP)]
    psum x1 -> x0, waiting for transfers between devices: 17.7 us -> none  [per_device(): summed = lax.psum(prods, 'mz')]
  transfers between devices with their start and end apart: 6 -> 6, of which waited for: 4 -> 5; matrix products, arithmetic and copies ran while one was open for 7% -> 1% of each run, Pallas kernels for 0% -> 0%
where the time goes in v1:
time: 226 us
  waiting for transfers between devices  153 us (68%)
  blocking collectives  28.5 us (13%)
  Pallas kernels  27.3 us (12%)
  starting transfers between devices  9.2 us (4%)
  local copies, waits for them, and re-layouts  4.52 us (2%)
  other arithmetic  2.69 us (1%)
    all_to_all x1, waiting for transfers between devices, per_device(): lax.all_to_all(spectra.reshape(count, rows, width), 'scan', 0, 0, tiled=T...  135 us
    all_to_all x2, blocking collectives, gathered(): return lax.all_to_all(copies, 'scan', 0, 0, tiled=True)  28.5 us
    all_to_all x1, waiting for transfers between devices, per_device(): pieces = lax.all_to_all(both, 'scan', 0, 0, tiled=True)  14.8 us
    pallas_call x1, Pallas kernels, per_device(): pl.pallas_call(functools.partial(second_kernel, scale, pad), grid=(count,...  13.7 us
    pallas_call x1, Pallas kernels, per_device(): pl.pallas_call(functools.partial(first_kernel, scale, pad), grid=(count,)...  13.6 us
    all_to_all x1, starting transfers between devices, per_device(): lax.all_to_all(spectra.reshape(count, rows, width), 'scan', 0, 0, tiled=T...  4.91 us
  transfers between devices with their start and end apart: 6, of which 5 were waited for; matrix products, arithmetic and copies ran while one was open for 1% of the time, Pallas kernels for 0%

profile of v1, /device:TPU:0, one launch (start us, length us, event | category | flops | bytes accessed | tf_op | source)
XLA Modules:
  0.0 225.6 jit_solution(15793093883693511762)
XLA Ops:
  0.6 0.9 dynamic-slice_convert_fusion
  1.5 16.0 %all_to_all.20.mine = bf16[8,64,256]{2,1,0:T(8,128)(2,1)S(1)} all-to-all(bf16[8,64,256]{2,1,0:T(8,128)(2,1)S(1)} %broadcast_in_dim.7), channel_id=1, replica_groups=mesh['slab'=2,'scan'=8,'mz'=2] {'scan'}, dimensions={0} | all-to-all | bytes 524288 | tf_op jit(solution)/shard_map/all_to_all | solution.py:141
  17.5 0.0 copy-start.1
  17.5 0.0 copy-start
  17.5 4.9 %all-to-all-start.1 = ((bf16[8,768,512]{2,1,0:T(8,128)(2,1)}), bf16[8,768,512]{2,1,0:T(8,128)(2,1)}, u32[]{:S(2)}, u32[]{:S(2)}) async-start(bf16[8,768,512]{2,1,0:T(8,128)(2,1)} %bitcast.10), calls=%async_computation.1 | async-start | bytes 12582912 | tf_op jit(solution)/shard_map/all_to_all | solution.py:160
  22.5 0.0 copy-done.1
  22.5 0.1 collective-permute-start
  22.5 0.0 copy-done
  22.6 1.2 copy.7.wt
  23.7 0.4 collective-permute-done.other
  24.1 0.0 copy-start.6
  24.1 135.1 %all-to-all-done.1.data = bf16[8,768,512]{2,1,0:T(8,128)(2,1)} async-done(((bf16[8,768,512]{2,1,0:T(8,128)(2,1)}), bf16[8,768,512]{2,1,0:T(8,128)(2,1)}, u32[]{:S(2)}, u32[]{:S(2)}) %all-to-all-start.1) | async-done | bytes 6291488 | tf_op jit(solution)/shard_map/all_to_all | solution.py:160
  159.1 0.0 copy-done.6
  159.1 0.0 copy-start.7
  159.1 0.0 copy-start.3
  159.1 0.0 copy-start.4
  159.1 13.6 %first.1 = f32[2,8,64,256]{3,2,1,0:T(8,128)} custom-call(s32[1]{0:T(128)} %bitcast.core, bf16[768,512]{1,0:T(8,128)(2,1)} %bitcast.11, bf16[512,768]{1,0:T(8,128)(2,1)} %copy.7.wt, bf16[8,64,256]{2,1,0:T(8,128)(2,1)} %copy-done.1, bf16[8,64,256]{2,1,0:T(8,128)(2,1)} %copy-done.6, bf16[8,768,512]{2,1,0:T(8,128)(2,1)} %all-to-all-done.1.data), custom_call_target="tpu_custom_call" | custom-call | flops 6442450944 | bytes 6291456 | tf_op jit(solution)/shard_map/first/pallas_call | solution.py:168
  172.8 1.1 dynamic-slice_bitcast_fusion
  173.9 0.1 collective-permute-start.1
  173.9 1.9 collective-permute-done.1
  175.8 1.9 bitcast_add_fusion
  177.7 3.6 %all-to-all-start.2 = ((f32[8,64,256]{2,1,0:T(8,128)}), f32[8,64,256]{2,1,0:T(8,128)S(1)}, u32[]{:S(2)}, u32[]{:S(2)}) async-start(f32[8,64,256]{2,1,0:T(8,128)} %bitcast_add_fusion), calls=%async_computation.2 | async-start | bytes 1048576 | tf_op jit(solution)/shard_map/all_to_all | solution.py:194
  181.4 0.0 copy-done.7
  181.4 14.8 %all-to-all-done.2 = f32[8,64,256]{2,1,0:T(8,128)S(1)} async-done(((f32[8,64,256]{2,1,0:T(8,128)}), f32[8,64,256]{2,1,0:T(8,128)S(1)}, u32[]{:S(2)}, u32[]{:S(2)}) %all-to-all-start.2) | async-done | bytes 524320 | tf_op jit(solution)/shard_map/all_to_all | solution.py:194
  196.3 0.0 copy-done.3
  196.3 0.1 fusion
  196.4 12.5 %all_to_all.21.mine = bf16[8,64,256]{2,1,0:T(8,128)(2,1)S(1)} all-to-all(bf16[8,64,256]{2,1,0:T(8,128)(2,1)S(1)} %broadcast_in_dim.8), channel_id=1, replica_groups=mesh['slab'=2,'scan'=8,'mz'=2] {'scan'}, dimensions={0} | all-to-all | bytes 524288 | tf_op jit(solution)/shard_map/all_to_all | solution.py:141
  208.9 0.0 copy-start.2
  208.9 0.0 collective-permute-start.3
  208.9 0.5 collective-permute-start.2
  209.4 0.0 copy-done.4
  209.4 0.7 broadcast_in_dim_tile.3.rates
  210.1 0.4 collective-permute-done.2
  210.5 0.7 maximum_select_fusion
  211.2 0.0 collective-permute-done.3.other
  211.2 0.0 copy-done.2
  211.2 0.0 copy-start.5
  211.2 0.7 copy-done.5
  211.9 13.7 %second.1 = bf16[768,512]{1,0:T(8,128)(2,1)} custom-call(s32[1]{0:T(128)} %bitcast.core, bf16[768,512]{1,0:T(8,128)(2,1)} %bitcast.12, f32[1,512]{1,0:T(1,128)} %broadcast_in_dim_tile.3.rates, bf16[8,64,256]{2,1,0:T(8,128)(2,1)} %copy-done.2, bf16[8,64,256]{2,1,0:T(8,128)(2,1)} %copy-done.5, bf16[8,768,512]{2,1,0:T(8,128)(2,1)} %all-to-all-done.1.data), custom_call_target="tpu_custom_call" | custom-call | flops 6442450944 | bytes 6291456 | tf_op jit(solution)/shard_map/second/pallas_call | solution.py:207
  (5 shorter events, 0.1 us)
Async XLA Ops:
  17.5 4.9 %copy-start.1 = (bf16[8,64,256]{2,1,0:T(8,128)(2,1)}, bf16[8,64,256]{2,1,0:T(8,128)(2,1)S(1)}, u32[]{:S(2)}) copy-start(bf16[8,64,256]{2,1,0:T(8,128)(2,1)S(1)} %all_to_all.20.mine) | copy-start | bytes 786436
  17.5 5.0 %copy-start = (bf16[1,768,512]{2,1,0:T(8,128)(2,1)S(1)}, bf16[1,768,512]{2,1,0:T(8,128)(2,1)}, u32[]{:S(2)}) copy-start(bf16[1,768,512]{2,1,0:T(8,128)(2,1)} %param.6) | copy-start | bytes 2359300
  17.5 141.6 %all-to-all-start.1 = ((bf16[8,768,512]{2,1,0:T(8,128)(2,1)}), bf16[8,768,512]{2,1,0:T(8,128)(2,1)}, u32[]{:S(2)}, u32[]{:S(2)}) async-start(bf16[8,768,512]{2,1,0:T(8,128)(2,1)} %bitcast.10), calls=%async_computation.1 | async-start | bytes 12582912 | tf_op jit(solution)/shard_map/all_to_all | solution.py:160
  22.5 1.6 collective-permute-start
  24.1 135.1 %copy-start.6 = (bf16[8,64,256]{2,1,0:T(8,128)(2,1)}, bf16[8,64,256]{2,1,0:T(8,128)(2,1)S(1)}, u32[]{:S(2)}) copy-start(bf16[8,64,256]{2,1,0:T(8,128)(2,1)S(1)} %collective-permute-done.other) | copy-start | bytes 786436
  159.1 22.2 %copy-start.7 = (f32[64]{0:T(128)S(1)}, f32[64]{0:T(128)}, u32[]{:S(2)}) copy-start(f32[64]{0:T(128)} %param.8) | copy-start | bytes 772
  159.1 37.1 %copy-start.3 = (f32[64,512]{1,0:T(8,128)S(1)}, f32[64,512]{1,0:T(8,128)}, u32[]{:S(2)}) copy-start(f32[64,512]{1,0:T(8,128)} %param.7) | copy-start | bytes 393220
  159.1 50.3 %copy-start.4 = (f32[64]{0:T(128)S(1)}, f32[64]{0:T(128)}, u32[]{:S(2)}) copy-start(f32[64]{0:T(128)} %param.9) | copy-start | bytes 772
  173.9 2.0 collective-permute-start.1
  177.7 18.5 %all-to-all-start.2 = ((f32[8,64,256]{2,1,0:T(8,128)}), f32[8,64,256]{2,1,0:T(8,128)S(1)}, u32[]{:S(2)}, u32[]{:S(2)}) async-start(f32[8,64,256]{2,1,0:T(8,128)} %bitcast_add_fusion), calls=%async_computation.2 | async-start | bytes 1048576 | tf_op jit(solution)/shard_map/all_to_all | solution.py:194
  208.9 2.3 %copy-start.2 = (bf16[8,64,256]{2,1,0:T(8,128)(2,1)}, bf16[8,64,256]{2,1,0:T(8,128)(2,1)S(1)}, u32[]{:S(2)}) copy-start(bf16[8,64,256]{2,1,0:T(8,128)(2,1)S(1)} %all_to_all.21.mine) | copy-start | bytes 786436
  208.9 2.3 %collective-permute-start.3 = (bf16[8,64,256]{2,1,0:T(8,128)(2,1)S(1)}, bf16[8,64,256]{2,1,0:T(8,128)(2,1)S(1)}, u32[]{:S(2)}, u32[]{:S(2)}) collective-permute-start(bf16[8,64,256]{2,1,0:T(8,128)(2,1)S(1)} %all_to_all.21.mine), channel_id=1, source_target_pairs={{0,1},{1,0},{2,3},{3,2},{4,5},{5,4},{6,7},{7,6},{8,9},{9,8},{10,11... | collective-permute-start | bytes 786440 | tf_op jit(solution)/shard_map/ppermute | solution.py:198
  208.9 1.6 collective-permute-start.2
  211.2 0.7 copy-start.5
